TPU v7x, 512 devices: a whole 4x8x8 slice. The times are simulated.
512 devices in a mesh: dp: 8 (over z), section: 4 (over x), patch: 16 (over y, core).
Axes of the slice: x: 4, y: 8, z: 8, core: 2. Of those that a mesh axis runs over, the one named last changes fastest.
Arguments:
- maps: bfloat16 [4, 8, 1536, 256], P(None, 'dp', 'patch'), may hold values from -6 to 6
- upstream: bfloat16 [4, 8, 1536, 256], P(None, 'dp', 'patch'), may hold values from -6 to 6
- weights: bfloat16 [4, 2304, 256], P('section'), may hold values from -0.125 to 0.125
- neighbours: int32 [9, 1536], P(None, 'patch'), may hold values from 0 to 1535, as said below
Outputs:
- input_grads: bfloat16 [4, 4, 8, 1536, 256], P('section', None, 'dp', 'patch')
- weight_grads: bfloat16 [4, 2304, 256], P('section')
Inputs may be any that keep to these rules, and one draw needn't show every extreme that they name: neighbours[0, p] = p; every entry is (p + d) mod 1536 with -32 <= d <= 32, and both d = 32 and d = -32 occur in every draw.
All inputs are finite; a program needn't handle non-finite values.
Results may differ from a plain program's by a relative error of at most 0.0063.
Values may be sent and summed in bfloat16 or wider, within the bound.
No kernel may reach another device: no remote copies, remote signals or barrier semaphores. Data moves between devices by JAX's collectives and lax.ppermute only.
A program may use at most 64 MiB of HBM per device.

v0:
```python
import jax
import jax.numpy as jnp
from jax import lax
from jax.sharding import PartitionSpec as P

HALO = 32


def extended_2(block, sides, width):
    for axis, dim in sides:
        count = lax.axis_size(axis)
        forward = [(i, i + 1) for i in range(count - 1)]
        forward.append((count - 1, 0))
        backward = [(target, source) for source, target in forward]
        low = lax.ppermute(
            lax.slice_in_dim(block, block.shape[dim] - width, None, axis=dim), axis, forward
        )
        high = lax.ppermute(lax.slice_in_dim(block, 0, width, axis=dim), axis, backward)
        block = jnp.concatenate([low, block, high], axis=dim)
    return block


def from_behind(shard, axis, by):
    size = lax.axis_size(axis)
    pairs = [(i, i + by) for i in range(size) if 0 <= i + by < size]
    return lax.ppermute(shard, axis, pairs)


def body(maps, upstream, weights, neighbours):
    micro = maps.shape[0]
    pix = maps.shape[2]
    chans = maps.shape[3]
    taps = neighbours.shape[0]
    sections = lax.axis_size("section")
    patches = lax.axis_size("patch")
    section_id = lax.axis_index("section")
    patch_id = lax.axis_index("patch")
    total = pix * patches
    local = jnp.mod(neighbours - patch_id * pix + HALO, total)
    index_rows = local.T.reshape(-1)
    w_flat = weights[0]
    w_taps = w_flat.reshape((taps, chans, chans))
    width = pix + 2 * HALO
    saved_ext = jnp.zeros((micro, width, chans), jnp.bfloat16)
    saved_tanh = jnp.zeros((micro, pix, chans), jnp.float32)
    incoming = jnp.zeros((pix, chans), jnp.bfloat16)
    for tick in range(micro + sections - 1):
        slot = tick - section_id
        valid = (slot >= 0) & (slot < micro)
        clipped = jnp.clip(slot, 0, micro - 1)
        current = jnp.where(section_id == 0, maps[min(tick, micro - 1), 0], incoming)
        extended = extended_2(current, (("patch", 0),), HALO)
        gathered = extended[index_rows].reshape((pix, taps * chans))
        act = jnp.dot(gathered, w_flat, preferred_element_type=jnp.float32)
        squash = jnp.tanh(act)
        result = (current.astype(jnp.float32) + squash).astype(jnp.bfloat16)
        saved_ext = saved_ext.at[clipped].set(jnp.where(valid, extended, saved_ext[clipped]))
        saved_tanh = saved_tanh.at[clipped].set(jnp.where(valid, squash, saved_tanh[clipped]))
        incoming = from_behind(result, "section", 1)
    grad_in = jnp.zeros((pix, chans), jnp.bfloat16)
    weight_acc = jnp.zeros((taps * chans, chans), jnp.float32)
    grads_out = jnp.zeros((micro, 1, pix, chans), jnp.bfloat16)
    for tick in range(micro + sections - 1):
        slot = tick - (sections - 1 - section_id)
        valid = (slot >= 0) & (slot < micro)
        clipped = jnp.clip(slot, 0, micro - 1)
        grad = jnp.where(section_id == sections - 1, upstream[min(tick, micro - 1), 0], grad_in)
        squash = saved_tanh[clipped]
        pre = (grad.astype(jnp.float32) * (1.0 - squash * squash)).astype(jnp.bfloat16)
        gathered = saved_ext[clipped][index_rows].reshape((pix, taps * chans))
        term = lax.dot_general(
            gathered, pre, (((0,), (0,)), ((), ())), preferred_element_type=jnp.float32
        )
        weight_acc = weight_acc + jnp.where(valid, term, 0.0)
        parts = jnp.einsum("qo,kio->qki", pre, w_taps, preferred_element_type=jnp.float32)
        spread = (
            jnp.zeros((width, chans), jnp.float32)
            .at[index_rows]
            .add(parts.reshape((pix * taps, chans)))
        )
        rims = jnp.concatenate([spread[:HALO], spread[pix + HALO :]], 0)
        returned = extended_2(rims, (("patch", 0),), HALO)
        own = spread[HALO : HALO + pix]
        own = own.at[:HALO].add(returned[:HALO])
        own = own.at[pix - HALO :].add(returned[3 * HALO :])
        dx_level = (grad.astype(jnp.float32) + own).astype(jnp.bfloat16)
        grads_out = grads_out.at[clipped, 0].set(jnp.where(valid, dx_level, grads_out[clipped, 0]))
        grad_in = from_behind(dx_level, "section", -1)
    summed = lax.psum(weight_acc, ("dp", "patch")).astype(jnp.bfloat16)
    return (grads_out[None], summed[None])


def solution(mesh):
    in_specs = (
        P(None, "dp", "patch", None),
        P(None, "dp", "patch", None),
        P("section", None, None),
        P(None, "patch"),
    )
    out_specs = (P("section", None, "dp", "patch", None), P("section", None, None))
    return jax.shard_map(body, mesh=mesh, in_specs=in_specs, out_specs=out_specs, check_vma=False)
```

profile of v0, /device:TPU:4, one launch (start us, length us, event | category | flops | bytes accessed | tf_op | source)
XLA Modules:
  0.0 830.5 jit_solution(4863639710440151621)
XLA Ops:
  16.0 3.5 gather_fusion
  21.1 3.1 collective-permute-start.2
  31.5 3.5 gather_fusion.1
  36.5 3.1 collective-permute-start.5
  39.6 4.6 collective-permute-done.5
  48.7 3.5 gather_fusion.2
  55.6 4.0 collective-permute-done.8
  64.1 3.5 gather_fusion.3
  71.0 4.0 collective-permute-done.11
  79.4 3.5 gather_fusion.4
  86.4 4.0 collective-permute-done.14
  94.8 3.5 gather_fusion.5
  101.9 3.9 collective-permute-done.17
  110.2 3.5 gather_fusion.6
  118.2 6.1 scatter_custom_fusion
  130.4 3.9 collective-permute-start.22
  134.4 3.5 gather_fusion.7
  143.9 6.1 scatter_custom_fusion.1
  159.4 3.5 gather_fusion.9
  164.1 3.5 gather_fusion.8
  168.9 3.5 gather_fusion.11
  173.6 3.5 gather_fusion.10
  178.3 3.5 gather_fusion.13
  183.1 3.5 gather_fusion.12
  189.9 6.1 scatter_custom_fusion.2
  196.9 3.0 collective-permute-start.27
  213.6 6.6 scatter_custom_fusion.3
  231.4 3.8 fusion.5
  239.1 6.1 scatter_custom_fusion.4
  265.4 6.6 scatter_custom_fusion.5
  294.4 6.6 scatter_custom_fusion.6
  302.5 522.8 %all-reduce.1 = bf16[2304,256]{1,0:T(8,128)(2,1)} all-reduce(f32[2304,256]{1,0:T(8,128)S(1)} %fusion.3), channel_id=1, replica_groups=mesh['dp'=8,'section'=4,'patch'=16] {'dp','patch'}, use_global_device_ids=true, to_apply=%region_21.22 | all-reduce | flops 589824 | bytes 3538944 | tf_op jit(solution)/shard_map/psum | solution.py:89
  (265 shorter events, 175.5 us)
Async XLA Ops:
  1.6 14.4 %collective-permute-start = (bf16[32,256]{1,0:T(8,128)(2,1)S(1)}, bf16[32,256]{1,0:T(8,128)(2,1)S(1)}, u32[]{:S(2)}, u32[]{:S(2)}) collective-permute-start(bf16[32,256]{1,0:T(8,128)(2,1)S(1)} %get-tuple-element.483), channel_id=1, source_target_pairs={{0,1},{1,2},{2,3},{3,4},{4,5},{5,6},{6,7},{7,8},{8,9},{9,10},{10,1... | collective-permute-start | bytes 49160 | tf_op jit(solution)/shard_map/ppermute | solution.py:15
  1.6 14.4 %collective-permute-start.1 = (bf16[32,256]{1,0:T(8,128)(2,1)S(1)}, bf16[32,256]{1,0:T(8,128)(2,1)S(1)}, u32[]{:S(2)}, u32[]{:S(2)}) collective-permute-start(bf16[32,256]{1,0:T(8,128)(2,1)S(1)} %get-tuple-element.484), channel_id=1, source_target_pairs={{1,0},{2,1},{3,2},{4,3},{5,4},{6,5},{7,6},{8,7},{9,8},{10,9},{11,1... | collective-permute-start | bytes 49160 | tf_op jit(solution)/shard_map/ppermute | solution.py:18
  21.1 6.0 collective-permute-start.2
  27.1 4.4 collective-permute-start.4
  36.5 7.7 collective-permute-start.5
  44.3 4.4 collective-permute-start.7
  53.6 6.0 collective-permute-start.8
  59.7 4.4 collective-permute-start.10
  69.0 6.0 collective-permute-start.11
  75.0 4.4 collective-permute-start.13
  84.4 6.0 collective-permute-start.14
  90.5 4.4 collective-permute-start.16
  99.8 6.0 collective-permute-start.17
  124.3 4.6 collective-permute-start.20
  124.3 4.5 collective-permute-start.21
  130.4 8.8 %collective-permute-start.22 = (bf16[96,256]{1,0:T(8,128)(2,1)S(1)}, bf16[96,256]{1,0:T(8,128)(2,1)S(1)}, u32[]{:S(2)}, u32[]{:S(2)}) collective-permute-start(bf16[96,256]{1,0:T(8,128)(2,1)S(1)} %get-tuple-element.449), channel_id=1, source_target_pairs={{16,0},{32,16},{48,32},{17,1},{33,17},{49,33},{18,2},{34,18},{50,3... | collective-permute-start | bytes 147464 | tf_op jit(solution)/shard_map/ppermute | solution.py:26
  150.0 4.6 collective-permute-start.23
  150.0 4.5 collective-permute-start.24
  155.3 32.5 %collective-permute-start.25 = (bf16[96,256]{1,0:T(8,128)(2,1)S(1)}, bf16[96,256]{1,0:T(8,128)(2,1)S(1)}, u32[]{:S(2)}, u32[]{:S(2)}) collective-permute-start(bf16[96,256]{1,0:T(8,128)(2,1)S(1)} %get-tuple-element.447), channel_id=1, source_target_pairs={{16,0},{32,16},{48,32},{17,1},{33,17},{49,33},{18,2},{34,18},{50,3... | collective-permute-start | bytes 147464 | tf_op jit(solution)/shard_map/ppermute | solution.py:26
  196.0 4.6 collective-permute-start.26
  196.9 4.5 collective-permute-start.27
  202.7 6.0 collective-permute-start.28
  221.0 4.7 collective-permute-start.29
  222.7 4.5 collective-permute-start.30
  229.4 6.0 collective-permute-start.31
  245.2 4.6 collective-permute-start.32
  246.1 4.5 collective-permute-start.33
  252.6 6.0 collective-permute-start.34
  272.8 4.7 collective-permute-start.35
  274.5 4.5 collective-permute-start.36
  281.2 6.1 collective-permute-start.37
  302.5 523.8 %collective-permute-start.38 = (f32[32,256]{1,0:T(8,128)}, f32[32,256]{1,0:T(8,128)}, u32[]{:S(2)}, u32[]{:S(2)}) collective-permute-start(f32[32,256]{1,0:T(8,128)} %get-tuple-element.458), channel_id=1, source_target_pairs={{0,1},{1,2},{2,3},{3,4},{4,5},{5,6},{6,7},{7,8},{8,9},{9,10},{10,1... | collective-permute-start | bytes 98312 | tf_op jit(solution)/shard_map/ppermute | solution.py:15
  (29 other events, 234.4 us)
where the time goes:
time: 841 us; the launch traced here: 830 us
  blocking collectives  523 us (62%)
  local copies, waits for them, and re-layouts  94.9 us (11%)
  other arithmetic  79 us (9%)
  starting transfers between devices  67.1 us (8%)
  waiting for transfers between devices  39.9 us (5%)
  matrix products  24.8 us (3%)
    psum x1, blocking collectives, body(): summed = lax.psum(weight_acc, ('dp', 'patch')).astype(jnp.bfloat16)  523 us
    scatter-add x7, other arithmetic, body(): spread = jnp.zeros((width, chans), jnp.float32).at[index_rows].add(parts....  44.2 us
    ppermute x14, starting transfers between devices, extended_2(): lax.ppermute(lax.slice_in_dim(block, 0, width, axis=dim), axis, backward)  38.3 us
    ppermute x12, starting transfers between devices, from_behind(): return lax.ppermute(shard, axis, pairs)  28.6 us
    ppermute x12, waiting for transfers between devices, from_behind(): return lax.ppermute(shard, axis, pairs)  27.6 us
    gather x7, local copies, waits for them, and re-layouts, body(): gathered = extended[index_rows].reshape((pix, taps * chans))  24.2 us
    gather x7, local copies, waits for them, and re-layouts, body(): gathered = saved_ext[clipped][index_rows].reshape((pix, taps * chans))  24.2 us
  transfers between devices with their start and end apart: 40, of which 25 were waited for; matrix products, arithmetic and copies ran while one was open for 9% of the time, Pallas kernels for 0%

commit v1 on v0

--- a/solution.py
+++ b/solution.py
@@ -86,7 +86,7 @@
         dx_level = (grad.astype(jnp.float32) + own).astype(jnp.bfloat16)
         grads_out = grads_out.at[clipped, 0].set(jnp.where(valid, dx_level, grads_out[clipped, 0]))
         grad_in = from_behind(dx_level, "section", -1)
-    summed = lax.psum(weight_acc, ("dp", "patch")).astype(jnp.bfloat16)
+    summed = lax.psum(lax.psum(weight_acc, "patch"), "dp").astype(jnp.bfloat16)
     return (grads_out[None], summed[None])
 
 

time: 841 us -> 507 us (0.60)
  the two profiles are of different devices: /device:TPU:4 before, /device:TPU:32 now
where the time goes in v1:
time: 507 us; the launch traced here: 497 us
  waiting for transfers between devices  144 us (28%)
  local copies, waits for them, and re-layouts  89.6 us (18%)
  other arithmetic  76.5 us (15%)
  starting transfers between devices  74.9 us (15%)
  blocking collectives  70.1 us (14%)
  matrix products  26.1 us (5%)
  between operations  15.5 us (3%)
    psum x1, waiting for transfers between devices, body(): summed = lax.psum(lax.psum(weight_acc, 'patch'), 'dp').astype(jnp.bfloat16)  112 us
    psum x1, blocking collectives, body(): summed = lax.psum(lax.psum(weight_acc, 'patch'), 'dp').astype(jnp.bfloat16)  70.1 us
    scatter-add x7, other arithmetic, body(): spread = jnp.zeros((width, chans), jnp.float32).at[index_rows].add(parts....  43.6 us
    ppermute x14, starting transfers between devices, extended_2(): lax.ppermute(lax.slice_in_dim(block, 0, width, axis=dim), axis, backward)  41.2 us
    ppermute x12, starting transfers between devices, from_behind(): return lax.ppermute(shard, axis, pairs)  33.4 us
    gather x7, local copies, waits for them, and re-layouts, body(): gathered = extended[index_rows].reshape((pix, taps * chans))  24.2 us
    gather x7, local copies, waits for them, and re-layouts, body(): gathered = saved_ext[clipped][index_rows].reshape((pix, taps * chans))  24.2 us
    ppermute x12, waiting for transfers between devices, from_behind(): return lax.ppermute(shard, axis, pairs)  19.2 us
  transfers between devices with their start and end apart: 41, of which 27 were waited for; matrix products, arithmetic and copies ran while one was open for 16% of the time, Pallas kernels for 0%

profile of v1, /device:TPU:32, one launch (start us, length us, event | category | flops | bytes accessed | tf_op | source)
XLA Modules:
  0.0 496.8 jit_solution(16115502438284134906)
XLA Ops:
  22.5 3.5 gather_fusion
  27.6 3.4 collective-permute-start.2
  37.1 3.5 gather_fusion.1
  42.1 4.2 collective-permute-start.5
  52.5 3.5 gather_fusion.2
  57.4 4.2 collective-permute-start.8
  67.8 3.5 gather_fusion.3
  72.8 4.2 collective-permute-start.11
  83.2 3.5 gather_fusion.4
  88.2 4.2 collective-permute-start.14
  98.6 3.5 gather_fusion.5
  103.6 4.4 collective-permute-start.17
  114.0 3.5 gather_fusion.6
  121.9 6.1 %scatter_custom_fusion = f32[160,256]{1,0:T(8,128)S(1)} fusion(s32[864]{0:T(1024)S(1)} %fusion.135, f32[864,256]{1,0:T(8,128)} %reshape.1365, f32[]{:T(128)} %constant.778.clone.1), kind=kCustom, calls=%fused_computation.152 | custom fusion | flops 221184 | bytes 164352 | tf_op jit(solution)/shard_map/scatter-add | solution.py:79
  135.4 3.5 gather_fusion.7
  145.1 6.1 %scatter_custom_fusion.1 = f32[160,256]{1,0:T(8,128)S(1)} fusion(s32[864]{0:T(1024)S(1)} %fusion.135, f32[864,256]{1,0:T(8,128)} %reshape.1373, f32[]{:T(128)} %constant.778.clone.1), kind=kCustom, calls=%fused_computation.150 | custom fusion | flops 221184 | bytes 164352 | tf_op jit(solution)/shard_map/scatter-add | solution.py:79
  159.9 3.5 gather_fusion.9
  164.6 3.5 gather_fusion.8
  169.4 3.5 gather_fusion.11
  174.1 3.5 gather_fusion.10
  178.9 3.5 gather_fusion.13
  183.6 3.5 gather_fusion.12
  190.4 6.1 %scatter_custom_fusion.2 = f32[160,256]{1,0:T(8,128)S(1)} fusion(s32[864]{0:T(1024)S(1)} %fusion.135, f32[864,256]{1,0:T(8,128)} %reshape.1381, f32[]{:T(128)} %constant.778.clone.1), kind=kCustom, calls=%fused_computation.148 | custom fusion | flops 221184 | bytes 164352 | tf_op jit(solution)/shard_map/scatter-add | solution.py:79
  197.4 3.0 collective-permute-start.27
  215.6 6.7 %scatter_custom_fusion.3 = f32[160,256]{1,0:T(8,128)} fusion(s32[864]{0:T(1024)S(1)} %fusion.135, f32[864,256]{1,0:T(8,128)} %reshape.1389, f32[]{:T(128)} %constant.778.clone.1), kind=kCustom, calls=%fused_computation.146 | custom fusion | flops 221184 | bytes 164352 | tf_op jit(solution)/shard_map/scatter-add | solution.py:79
  232.7 3.8 fusion.5
  241.1 6.1 %scatter_custom_fusion.4 = f32[160,256]{1,0:T(8,128)S(1)} fusion(s32[864]{0:T(1024)S(1)} %fusion.135, f32[864,256]{1,0:T(8,128)} %reshape.1397, f32[]{:T(128)} %constant.778.clone.1), kind=kCustom, calls=%fused_computation.144 | custom fusion | flops 221184 | bytes 164352 | tf_op jit(solution)/shard_map/scatter-add | solution.py:79
  257.7 3.0 collective-permute-done.34
  267.5 6.6 %scatter_custom_fusion.5 = f32[160,256]{1,0:T(8,128)} fusion(s32[864]{0:T(1024)S(1)} %fusion.135, f32[864,256]{1,0:T(8,128)} %reshape.1405, f32[]{:T(128)} %constant.778.clone.1), kind=kCustom, calls=%fused_computation.142 | custom fusion | flops 221184 | bytes 164352 | tf_op jit(solution)/shard_map/scatter-add | solution.py:79
  295.5 6.1 %scatter_custom_fusion.6 = f32[160,256]{1,0:T(8,128)S(1)} fusion(s32[864]{0:T(1024)S(1)} %fusion.135, f32[864,256]{1,0:T(8,128)} %reshape.1413, f32[]{:T(128)} %constant.778.clone.1), kind=kCustom, calls=%fused_computation.140 | custom fusion | flops 221184 | bytes 164352 | tf_op jit(solution)/shard_map/scatter-add | solution.py:79
  307.7 112.0 %all-reduce.3.cloned.1.call-done = f32[2304,256]{1,0:T(8,128)} async-done(((f32[2304,256]{1,0:T(8,128)}), f32[2304,256]{1,0:T(8,128)}) %all-reduce.3.cloned.1.call-update) | async-done | bytes 2359312 | tf_op jit(solution)/shard_map/psum | solution.py:89
  419.7 70.1 %all-reduce.4 = bf16[2304,256]{1,0:T(8,128)(2,1)} all-reduce(f32[2304,256]{1,0:T(8,128)} %all-reduce.3.cloned.1.call-done), channel_id=1, replica_groups=mesh['dp'=8,'section'=4,'patch'=16] {'dp'}, use_global_device_ids=true, to_apply=%region_22.23 | all-reduce | flops 589824 | bytes 3538944 | tf_op jit(solution)/shard_map/psum | solution.py:89
  (272 shorter events, 172.6 us)
Async XLA Ops:
  7.2 412.5 %all-reduce.3.cloned.1.call-start = ((), (), s32[]{:S(2)}) async-start(), calls=%async_computation | async-start | bytes 4718592 | tf_op jit(solution)/shard_map/psum | solution.py:89
  8.1 14.3 %collective-permute-start = (bf16[32,256]{1,0:T(8,128)(2,1)S(1)}, bf16[32,256]{1,0:T(8,128)(2,1)S(1)}, u32[]{:S(2)}, u32[]{:S(2)}) collective-permute-start(bf16[32,256]{1,0:T(8,128)(2,1)S(1)} %get-tuple-element.483), channel_id=1, source_target_pairs={{0,1},{1,2},{2,3},{3,4},{4,5},{5,6},{6,7},{7,8},{8,9},{9,10},{10,1... | collective-permute-start | bytes 49160 | tf_op jit(solution)/shard_map/ppermute | solution.py:15
  8.2 14.3 %collective-permute-start.1 = (bf16[32,256]{1,0:T(8,128)(2,1)S(1)}, bf16[32,256]{1,0:T(8,128)(2,1)S(1)}, u32[]{:S(2)}, u32[]{:S(2)}) collective-permute-start(bf16[32,256]{1,0:T(8,128)(2,1)S(1)} %get-tuple-element.484), channel_id=1, source_target_pairs={{1,0},{2,1},{3,2},{4,3},{5,4},{6,5},{7,6},{8,7},{9,8},{10,9},{11,1... | collective-permute-start | bytes 49160 | tf_op jit(solution)/shard_map/ppermute | solution.py:18
  27.6 5.1 %collective-permute-start.2 = (bf16[96,256]{1,0:T(8,128)(2,1)S(1)}, bf16[96,256]{1,0:T(8,128)(2,1)S(1)}, u32[]{:S(2)}, u32[]{:S(2)}) collective-permute-start(bf16[96,256]{1,0:T(8,128)(2,1)S(1)} %add_convert_fusion.5), channel_id=1, source_target_pairs={{0,16},{16,32},{32,48},{1,17},{17,33},{33,49},{2,18},{18,34},{34,5... | collective-permute-start | bytes 147464 | tf_op jit(solution)/shard_map/ppermute | solution.py:26
  32.7 4.4 collective-permute-start.4
  42.1 6.0 %collective-permute-start.5 = (bf16[96,256]{1,0:T(8,128)(2,1)S(1)}, bf16[96,256]{1,0:T(8,128)(2,1)S(1)}, u32[]{:S(2)}, u32[]{:S(2)}) collective-permute-start(bf16[96,256]{1,0:T(8,128)(2,1)S(1)} %add_convert_fusion.4), channel_id=1, source_target_pairs={{0,16},{16,32},{32,48},{1,17},{17,33},{33,49},{2,18},{18,34},{34,5... | collective-permute-start | bytes 147464 | tf_op jit(solution)/shard_map/ppermute | solution.py:26
  48.1 4.4 collective-permute-start.7
  57.4 6.0 %collective-permute-start.8 = (bf16[96,256]{1,0:T(8,128)(2,1)S(1)}, bf16[96,256]{1,0:T(8,128)(2,1)S(1)}, u32[]{:S(2)}, u32[]{:S(2)}) collective-permute-start(bf16[96,256]{1,0:T(8,128)(2,1)S(1)} %add_convert_fusion.3), channel_id=1, source_target_pairs={{0,16},{16,32},{32,48},{1,17},{17,33},{33,49},{2,18},{18,34},{34,5... | collective-permute-start | bytes 147464 | tf_op jit(solution)/shard_map/ppermute | solution.py:26
  72.8 6.0 %collective-permute-start.11 = (bf16[96,256]{1,0:T(8,128)(2,1)S(1)}, bf16[96,256]{1,0:T(8,128)(2,1)S(1)}, u32[]{:S(2)}, u32[]{:S(2)}) collective-permute-start(bf16[96,256]{1,0:T(8,128)(2,1)S(1)} %add_convert_fusion.2), channel_id=1, source_target_pairs={{0,16},{16,32},{32,48},{1,17},{17,33},{33,49},{2,18},{18,34},{34,5... | collective-permute-start | bytes 147464 | tf_op jit(solution)/shard_map/ppermute | solution.py:26
  78.8 4.4 collective-permute-start.13
  88.2 6.0 %collective-permute-start.14 = (bf16[96,256]{1,0:T(8,128)(2,1)S(1)}, bf16[96,256]{1,0:T(8,128)(2,1)S(1)}, u32[]{:S(2)}, u32[]{:S(2)}) collective-permute-start(bf16[96,256]{1,0:T(8,128)(2,1)S(1)} %add_convert_fusion.1), channel_id=1, source_target_pairs={{0,16},{16,32},{32,48},{1,17},{17,33},{33,49},{2,18},{18,34},{34,5... | collective-permute-start | bytes 147464 | tf_op jit(solution)/shard_map/ppermute | solution.py:26
  103.6 6.0 %collective-permute-start.17 = (bf16[96,256]{1,0:T(8,128)(2,1)S(1)}, bf16[96,256]{1,0:T(8,128)(2,1)S(1)}, u32[]{:S(2)}, u32[]{:S(2)}) collective-permute-start(bf16[96,256]{1,0:T(8,128)(2,1)S(1)} %add_convert_fusion), channel_id=1, source_target_pairs={{0,16},{16,32},{32,48},{1,17},{17,33},{33,49},{2,18},{18,34},{34,5... | collective-permute-start | bytes 147464 | tf_op jit(solution)/shard_map/ppermute | solution.py:26
  128.0 4.6 collective-permute-start.20
  128.0 4.5 collective-permute-start.21
  134.0 6.3 %collective-permute-start.22 = (bf16[96,256]{1,0:T(8,128)(2,1)S(1)}, bf16[96,256]{1,0:T(8,128)(2,1)S(1)}, u32[]{:S(2)}, u32[]{:S(2)}) collective-permute-start(bf16[96,256]{1,0:T(8,128)(2,1)S(1)} %get-tuple-element.449), channel_id=1, source_target_pairs={{16,0},{32,16},{48,32},{17,1},{33,17},{49,33},{18,2},{34,18},{50,3... | collective-permute-start | bytes 147464 | tf_op jit(solution)/shard_map/ppermute | solution.py:26
  151.2 4.6 collective-permute-start.23
  151.2 4.5 collective-permute-start.24
  156.4 31.8 %collective-permute-start.25 = (bf16[96,256]{1,0:T(8,128)(2,1)S(1)}, bf16[96,256]{1,0:T(8,128)(2,1)S(1)}, u32[]{:S(2)}, u32[]{:S(2)}) collective-permute-start(bf16[96,256]{1,0:T(8,128)(2,1)S(1)} %get-tuple-element.447), channel_id=1, source_target_pairs={{16,0},{32,16},{48,32},{17,1},{33,17},{49,33},{18,2},{34,18},{50,3... | collective-permute-start | bytes 147464 | tf_op jit(solution)/shard_map/ppermute | solution.py:26
  196.5 4.6 collective-permute-start.26
  197.4 4.6 collective-permute-start.27
  203.2 7.4 %collective-permute-start.28 = (bf16[96,256]{1,0:T(8,128)(2,1)S(1)}, bf16[96,256]{1,0:T(8,128)(2,1)S(1)}, u32[]{:S(2)}, u32[]{:S(2)}) collective-permute-start(bf16[96,256]{1,0:T(8,128)(2,1)S(1)} %get-tuple-element.445), channel_id=1, source_target_pairs={{16,0},{32,16},{48,32},{17,1},{33,17},{49,33},{18,2},{34,18},{50,3... | collective-permute-start | bytes 147464 | tf_op jit(solution)/shard_map/ppermute | solution.py:26
  223.0 4.7 collective-permute-start.29
  224.7 4.5 collective-permute-start.30
  231.4 6.0 %collective-permute-start.31 = (bf16[96,256]{1,0:T(8,128)(2,1)S(1)}, bf16[96,256]{1,0:T(8,128)(2,1)S(1)}, u32[]{:S(2)}, u32[]{:S(2)}) collective-permute-start(bf16[96,256]{1,0:T(8,128)(2,1)S(1)} %get-tuple-element.443), channel_id=1, source_target_pairs={{16,0},{32,16},{48,32},{17,1},{33,17},{49,33},{18,2},{34,18},{50,3... | collective-permute-start | bytes 147464 | tf_op jit(solution)/shard_map/ppermute | solution.py:26
  247.1 4.6 collective-permute-start.32
  248.0 4.5 collective-permute-start.33
  254.7 6.0 %collective-permute-start.34 = (bf16[96,256]{1,0:T(8,128)(2,1)S(1)}, bf16[96,256]{1,0:T(8,128)(2,1)S(1)}, u32[]{:S(2)}, u32[]{:S(2)}) collective-permute-start(bf16[96,256]{1,0:T(8,128)(2,1)S(1)} %get-tuple-element.441), channel_id=1, source_target_pairs={{16,0},{32,16},{48,32},{17,1},{33,17},{49,33},{18,2},{34,18},{50,3... | collective-permute-start | bytes 147464 | tf_op jit(solution)/shard_map/ppermute | solution.py:26
  274.9 4.7 collective-permute-start.35
  276.6 4.5 collective-permute-start.36
  283.2 6.1 %collective-permute-start.37 = (bf16[96,256]{1,0:T(8,128)(2,1)S(1)}, bf16[96,256]{1,0:T(8,128)(2,1)S(1)}, u32[]{:S(2)}, u32[]{:S(2)}) collective-permute-start(bf16[96,256]{1,0:T(8,128)(2,1)S(1)} %get-tuple-element.439), channel_id=1, source_target_pairs={{16,0},{32,16},{48,32},{17,1},{33,17},{49,33},{18,2},{34,18},{50,3... | collective-permute-start | bytes 147464 | tf_op jit(solution)/shard_map/ppermute | solution.py:26
  301.6 4.6 collective-permute-start.38
  301.6 4.5 collective-permute-start.39
  (32 other events, 445.2 us)
Sparse Core Ops, SparseCore 0:
  293.5 126.1 all-reduce.2
